TPU v7x, 32 devices: a whole 2x2x4 slice. The times are simulated.
32 devices in a mesh: dp: 4 (over y, core), seq: 8 (over z, x).
Axes of the slice: x: 2, y: 2, z: 4, core: 2. Of those that a mesh axis runs over, the one named last changes fastest.
Arguments:
- tokens: bfloat16 [4, 24, 256, 1280], P('dp', 'seq'), may hold values from -6 to 6
- clip_ids: int32 [4, 24], P('dp'), may hold values from 0 to 5, never falling along the last dimension, each value on 1 to 12 neighbouring positions
- ln_gain: float32 [1280], replicated, may hold values from 0.1 to 1.9
- w_qkv: bfloat16 [1280, 1920], P(None, 'dp'), may hold values from -0.15625 to 0.15625
- w_out: bfloat16 [640, 1280], P(None, 'dp'), may hold values from -0.25 to 0.25
Outputs:
- output: bfloat16 [4, 24, 256, 1280], P('dp', 'seq')
Inputs may be any that keep to these rules, and one draw needn't show every extreme that they name: `clip_ids`: in each batch the clip numbers never fall along the frames, every clip number occurs, each clip covers 1 to 12 consecutive frames, and some clip covers exactly 12.
All inputs are finite; a program needn't handle non-finite values.
Results may differ from a plain program's by a relative error of at most 0.006.
Values may be sent and summed in bfloat16 or wider, within the bound.
A program may use at most 64 MiB of HBM per device.

v0:
```python
import math
import jax
import jax.numpy as jnp
from jax import lax
from jax.sharding import PartitionSpec as P

HS = 80
HEADS = 8
HD = 640
norm_eps = 1e-05


def layer_norm(block, ln_gain):
    values = block.astype(jnp.float32)
    center = jnp.mean(values, axis=-1, keepdims=True)
    spread = jnp.mean(jnp.square(values - center), axis=-1, keepdims=True)
    return ((values - center) * lax.rsqrt(spread + norm_eps) * ln_gain).astype(jnp.bfloat16)


def split_heads(projected):
    queries = (projected[:, :HD] * (1.0 / math.sqrt(HS))).astype(jnp.bfloat16)
    keys = projected[:, HD : 2 * HD].astype(jnp.bfloat16)
    values = projected[:, 2 * HD :].astype(jnp.bfloat16)
    return (queries, keys, values)


def attend(queries, keys, values, clip_row):
    scores = jnp.einsum("flhe,glhe->lhfg", queries, keys, preferred_element_type=jnp.float32)
    same_clip = clip_row[:, None] == clip_row[None, :]
    raised = jnp.where(same_clip, jnp.exp(scores), jnp.zeros_like(scores))
    attn_probs = (raised / jnp.sum(raised, axis=-1, keepdims=True)).astype(jnp.bfloat16)
    return jnp.einsum(
        "lhfg,glhe->flhe", attn_probs, values, preferred_element_type=jnp.float32
    ).astype(jnp.bfloat16)


def shards(tokens, clip_ids, ln_gain, w_qkv, w_out):
    width = tokens.shape[3]
    clip_row = clip_ids[0]
    frames = clip_row.shape[0]
    local_frames = tokens.shape[1]
    patches = tokens.shape[2]
    moved = lax.all_to_all(tokens, "seq", split_axis=2, concat_axis=1, tiled=True)
    places = moved.shape[2]
    normed = layer_norm(moved, ln_gain).reshape(frames * places, width)

    def column_block(piece, start):
        return jnp.dot(normed, piece, preferred_element_type=jnp.float32)

    queries, keys, values = split_heads(
        column_block(lax.all_gather(w_qkv, "dp", axis=1, tiled=True), jnp.int32(0))
    )
    head_shape = (frames, places, HEADS, HS)
    mixed = attend(
        queries.reshape(head_shape), keys.reshape(head_shape), values.reshape(head_shape), clip_row
    )
    mixed = lax.all_to_all(
        mixed.reshape(1, frames, places, HD), "seq", split_axis=1, concat_axis=2, tiled=True
    )
    row_count = local_frames * patches
    rows_in = mixed.reshape(row_count, HD)

    def column_block(piece, start):
        return jnp.dot(rows_in, piece, preferred_element_type=jnp.float32)

    update = column_block(lax.all_gather(w_out, "dp", axis=1, tiled=True), jnp.int32(0))
    summed = tokens.reshape(row_count, width).astype(jnp.float32) + update
    return summed.astype(jnp.bfloat16).reshape(tokens.shape)


def solution(mesh):
    placed = (P("dp", "seq", None, None), P("dp", None), P(), P(None, "dp"), P(None, "dp"))
    return jax.shard_map(
        shards, mesh=mesh, in_specs=placed, out_specs=P("dp", "seq", None, None), check_vma=False
    )
```

profile of v0, /device:TPU:0, one launch (start us, length us, event | category | flops | bytes accessed | tf_op | source)
XLA Modules:
  0.0 151.9 jit_solution(18149255715372341711)
XLA Ops:
  6.5 0.0 all-gather.3.cloned.1.call-start
  6.5 0.7 all-gather.3.cloned.1.call-update
  7.3 4.8 %copy.35 = bf16[1,3,256,1280]{3,1,0,2:T(4,128)(2,1)} copy(bf16[1,3,256,1280]{3,2,1,0:T(8,128)(2,1)} %param.5) | data formatting | bytes 3932160 | tf_op args[0]
  12.0 0.0 copy-start.2
  12.0 7.4 %all-to-all-start = ((bf16[1,3,256,1280]{3,1,0,2:T(4,128)(2,1)}), bf16[1,3,256,1280]{3,1,0,2:T(4,128)(2,1)S(1)}, u32[]{:S(2)}, u32[]{:S(2)}) async-start(bf16[1,3,256,1280]{3,1,0,2:T(4,128)(2,1)} %copy.35), calls=%async_computation | async-start | bytes 5242880 | tf_op jit(solution)/shard_map/all_to_all | solution.py:43
  19.4 0.0 all-gather.5.cloned.1.call-start
  19.5 0.7 all-gather.5.cloned.1.call-update
  20.2 0.0 copy-done.2
  20.2 0.1 broadcast_compare_fusion
  20.3 58.6 %all-to-all-done = bf16[1,3,256,1280]{3,1,0,2:T(4,128)(2,1)S(1)} async-done(((bf16[1,3,256,1280]{3,1,0,2:T(4,128)(2,1)}), bf16[1,3,256,1280]{3,1,0,2:T(4,128)(2,1)S(1)}, u32[]{:S(2)}, u32[]{:S(2)}) %all-to-all-start) | async-done | bytes 1966112 | tf_op jit(solution)/shard_map/all_to_all | solution.py:43
  78.9 2.3 %convert_bitcast_fusion = (f32[1,8,3,32,1280]{4,3,1,2,0:T(8,128)}, bf16[1,3,256,1280]{3,2,1,0:T(8,128)(2,1)S(1)}) fusion(bf16[1,3,256,1280]{3,1,0,2:T(4,128)(2,1)S(1)} %all-to-all-done), kind=kLoop, calls=%fused_computation.1 | loop fusion | flops 983040 | bytes 7864320 | tf_op jit(solution)/shard_map/convert_element_type | solution.py:14
  81.2 0.3 fusion.5
  81.6 0.7 multiply_reduce_fusion
  82.3 0.1 rsqrt.12
  82.4 0.1 div.17
  82.4 0.0 copy-start.1
  82.4 2.4 %copy.37 = f32[1,8,3,32,1280]{4,3,2,1,0:T(8,128)S(1)} copy(f32[1,8,3,32,1280]{4,3,1,2,0:T(8,128)} %get-tuple-element.5) | data formatting | bytes 7864320 | tf_op jit(solution)/shard_map/convert_element_type | solution.py:14
  84.9 0.0 copy-done.1
  84.9 0.6 fusion.2
  85.4 0.0 all-gather.3.cloned.1.call-done
  85.5 8.5 %fusion.18 = (bf16[768,1920]{1,0:T(8,128)(2,1)S(1)}, f32[768,1920]{1,0:T(8,128)}) fusion(bf16[768,1280]{1,0:T(8,128)(2,1)S(1)} %fusion.2, bf16[1280,1920]{0,1:T(8,128)(2,1)} %all-gather.3.cloned.1.call-done), kind=kOutput, calls=%fused_computation.27 | convolution fusion | flops 3776348160 | bytes 15728640 | tf_op jit(solution)/shard_map/dot_general | solution.py:48
  94.0 0.2 fusion.17
  94.2 1.6 %reshape.90 = bf16[24,32,8,80]{3,2,1,0:T(8,128)(2,1)S(1)} reshape(bf16[768,640]{1,0:T(8,128)(2,1)S(1)} %get-tuple-element.8) | data formatting | bytes 1966080 | tf_op jit(solution)/shard_map/reshape | solution.py:55
  95.8 1.7 %fusion.6 = bf16[768,640]{1,0:T(8,128)(2,1)S(1)} fusion(f32[768,1920]{1,0:T(8,128)} %get-tuple-element.10), kind=kLoop, calls=%fused_computation.13 | loop fusion | flops 983040 | bytes 2949120 | tf_op jit(solution)/shard_map/convert_element_type | solution.py:21
  97.5 2.5 %reshape.89 = bf16[24,32,8,80]{3,2,1,0:T(8,128)(2,1)} reshape(bf16[768,640]{1,0:T(8,128)(2,1)S(1)} %fusion.6) | data formatting | bytes 1966080 | tf_op jit(solution)/shard_map/reshape | solution.py:55
  100.0 5.7 %fusion.4 = (f32[32,8,24]{2,1,0:T(8,128)S(1)}, f32[32,8,24,24]{2,3,1,0:T(8,128)}) fusion(pred[24,24]{0,1:T(8,128)(4,1)S(1)} %broadcast_compare_fusion, bf16[24,32,8,80]{3,2,1,0:T(8,128)(2,1)S(1)} %reshape.90, bf16[24,32,8,80]{3,2,1,0:T(8,128)(2,1)} %reshape.89), kind=kOutput, calls=%fused_computation.10 | convolution fusion | flops 23881728 | bytes 2581056 | tf_op jit(solution)/shard_map/flhe,glhe->lhfg/dot_general | solution.py:28
  105.7 1.6 %reshape.88 = bf16[24,32,8,80]{3,2,1,0:T(8,128)(2,1)S(1)} reshape(bf16[768,640]{1,0:T(8,128)(2,1)S(1)} %get-tuple-element.7) | data formatting | bytes 1966080 | tf_op jit(solution)/shard_map/reshape | solution.py:55
  107.3 3.4 %fusion.13 = bf16[24,32,8,80]{3,0,2,1:T(8,128)(2,1)S(1)} fusion(f32[32,8,24,24]{2,3,1,0:T(8,128)} %get-tuple-element.12, f32[32,8,24]{2,1,0:T(8,128)S(1)} %get-tuple-element.11, pred[24,24]{0,1:T(8,128)(4,1)S(1)} %broadcast_compare_fusion, bf16[24,32,8,80]{3,2,1,0:T(8,128)(2,1)S(1)} %reshape.88), kind=kOutput, calls=%fused_computation.21 | convolution fusion | flops 24526848 | bytes 2581056 | tf_op jit(solution)/shard_map/lhfg,glhe->flhe/dot_general | solution.py:32
  110.7 0.3 copy.44
  111.1 1.2 reshape.91
  112.3 0.0 copy-start
  112.3 28.2 %all_to_all.24 = bf16[1,24,32,640]{3,2,0,1:T(8,128)(2,1)S(1)} all-to-all(bf16[1,24,32,640]{3,2,0,1:T(8,128)(2,1)S(1)} %bitcast.36), channel_id=1, replica_groups=mesh['dp'=4,'seq'=8] {'seq'}, dimensions={1} | all-to-all | bytes 1966080 | tf_op jit(solution)/shard_map/all_to_all | solution.py:57
  140.5 0.1 copy.46
  140.6 0.0 all-gather.5.cloned.1.call-done
  140.6 0.0 copy-done
  140.6 4.4 %fusion.3 = bf16[768,1280]{1,0:T(8,128)(2,1)} fusion(bf16[768,640]{1,0:T(8,128)(2,1)S(1)} %bitcast.39, bf16[640,1280]{0,1:T(8,128)(2,1)} %all-gather.5.cloned.1.call-done, bf16[768,1280]{1,0:T(8,128)(2,1)S(1)} %bitcast.38), kind=kOutput, calls=%fused_computation.7 | convolution fusion | flops 1261240320 | bytes 6553600 | tf_op jit(solution)/shard_map/dot_general | solution.py:64
  (4 shorter events, 0.0 us)
Async XLA Ops:
  6.5 78.9 %all-gather.3.cloned.1.call-start = ((), (), s32[]{:S(2)}) async-start(), calls=%async_computation.2 | async-start | bytes 6144000 | tf_op jit(solution)/shard_map/all_gather | solution.py:51
  12.0 8.2 %copy-start.2 = (s32[1,24]{1,0:T(1,128)S(1)}, s32[1,24]{1,0:T(1,128)}, u32[]{:S(2)}) copy-start(s32[1,24]{1,0:T(1,128)} %param.6) | copy-start | bytes 292
  12.0 66.9 %all-to-all-start = ((bf16[1,3,256,1280]{3,1,0,2:T(4,128)(2,1)}), bf16[1,3,256,1280]{3,1,0,2:T(4,128)(2,1)S(1)}, u32[]{:S(2)}, u32[]{:S(2)}) async-start(bf16[1,3,256,1280]{3,1,0,2:T(4,128)(2,1)} %copy.35), calls=%async_computation | async-start | bytes 5242880 | tf_op jit(solution)/shard_map/all_to_all | solution.py:43
  19.4 121.2 %all-gather.5.cloned.1.call-start = ((), (), s32[]{:S(2)}) async-start(), calls=%async_computation.3 | async-start | bytes 2048000 | tf_op jit(solution)/shard_map/all_gather | solution.py:66
  82.4 2.4 %copy-start.1 = (f32[1280]{0:T(1024)S(1)}, f32[1280]{0:T(1024)}, u32[]{:S(2)}) copy-start(f32[1280]{0:T(1024)} %param.7) | copy-start | bytes 15364
  112.3 28.3 %copy-start = (bf16[1,3,256,1280]{3,2,1,0:T(8,128)(2,1)S(1)}, bf16[1,3,256,1280]{3,2,1,0:T(8,128)(2,1)}, u32[]{:S(2)}) copy-start(bf16[1,3,256,1280]{3,2,1,0:T(8,128)(2,1)} %param.5) | copy-start | bytes 5898244
Sparse Core Ops, SparseCore 0:
  8.9 41.2 all-gather.2
  51.8 19.9 all-gather.4
where the time goes:
time: 152 us
  waiting for transfers between devices  60.1 us (40%)
  blocking collectives  28.2 us (19%)
  matrix products  22 us (14%)
  local copies, waits for them, and re-layouts  14.9 us (10%)
  between operations  13.6 us (9%)
  starting transfers between devices  7.45 us (5%)
  other arithmetic  5.69 us (4%)
    all_to_all x1, waiting for transfers between devices, shards(): lax.all_to_all(tokens, 'seq', split_axis=2, concat_axis=1, tiled=True)  58.6 us
    all_to_all x1, blocking collectives, shards(): lax.all_to_all(mixed.reshape(1, frames, places, HD), 'seq', split_axis=1,...  28.2 us
    dot_general x1, matrix products, column_block(): return jnp.dot(normed, piece, preferred_element_type=jnp.float32)  8.52 us
    all_to_all x1, starting transfers between devices, shards(): lax.all_to_all(tokens, 'seq', split_axis=2, concat_axis=1, tiled=True)  7.41 us
    dot_general x1, matrix products, attend(): jnp.einsum('flhe,glhe->lhfg', queries, keys, preferred_element_type=jnp.f...  5.69 us
    unnamed x7, local copies, waits for them, and re-layouts  4.77 us
    dot_general x1, matrix products, column_block(): return jnp.dot(rows_in, piece, preferred_element_type=jnp.float32)  4.43 us
    dot_general x1, matrix products, attend(): jnp.einsum('lhfg,glhe->flhe', attn_probs, values, preferred_element_type=...  3.4 us
  transfers between devices with their start and end apart: 3, of which 1 were waited for; matrix products, arithmetic and copies ran while one was open for 25% of the time, Pallas kernels for 0%

commit v1 on v0

--- a/solution.py
+++ b/solution.py
@@ -40,7 +40,10 @@
     frames = clip_row.shape[0]
     local_frames = tokens.shape[1]
     patches = tokens.shape[2]
-    moved = lax.all_to_all(tokens, "seq", split_axis=2, concat_axis=1, tiled=True)
+    size = lax.axis_size("seq")
+    pieces = jnp.stack(jnp.split(tokens, size, axis=2), axis=0)
+    pieces = lax.all_to_all(pieces, "seq", split_axis=0, concat_axis=0)
+    moved = jnp.concatenate(pieces, axis=1)
     places = moved.shape[2]
     normed = layer_norm(moved, ln_gain).reshape(frames * places, width)
 

time: 152 us -> 140 us (0.921)
  waiting for transfers between devices: 60.1 us -> 46 us
  local copies, waits for them, and re-layouts: 14.9 us -> 16.7 us
    all_to_all x1, waiting for transfers between devices: 58.6 us -> 44.6 us  [shards(): pieces = lax.all_to_all(pieces, 'seq', split_axis=0, concat_axis=0)]
    unnamed x7 -> x15, local copies, waits for them, and re-layouts: 4.77 us -> 8.28 us
    convert_element_type x1 -> x0, local copies, waits for them, and re-layouts: 2.42 us -> none  [layer_norm(): values = block.astype(jnp.float32)]
    convert_element_type x1 -> x0, other arithmetic: 2.34 us -> none  [layer_norm(): values = block.astype(jnp.float32)]
  transfers between devices with their start and end apart: 3 -> 3, of which waited for: 1 -> 1; matrix products, arithmetic and copies ran while one was open for 25% -> 28% of each run, Pallas kernels for 0% -> 0%
where the time goes in v1:
time: 140 us
  waiting for transfers between devices  46 us (33%)
  blocking collectives  28.1 us (20%)
  matrix products  23.4 us (17%)
  local copies, waits for them, and re-layouts  16.7 us (12%)
  between operations  13.5 us (10%)
  starting transfers between devices  7.45 us (5%)
  other arithmetic  4.74 us (3%)
    all_to_all x1, waiting for transfers between devices, shards(): pieces = lax.all_to_all(pieces, 'seq', split_axis=0, concat_axis=0)  44.6 us
    all_to_all x1, blocking collectives, shards(): lax.all_to_all(mixed.reshape(1, frames, places, HD), 'seq', split_axis=1,...  28.1 us
    dot_general x1, matrix products, column_block(): return jnp.dot(normed, piece, preferred_element_type=jnp.float32)  9.78 us
    unnamed x15, local copies, waits for them, and re-layouts  8.28 us
    all_to_all x1, starting transfers between devices, shards(): pieces = lax.all_to_all(pieces, 'seq', split_axis=0, concat_axis=0)  7.41 us
    dot_general x1, matrix products, attend(): jnp.einsum('flhe,glhe->lhfg', queries, keys, preferred_element_type=jnp.f...  5.73 us
    dot_general x1, matrix products, column_block(): return jnp.dot(rows_in, piece, preferred_element_type=jnp.float32)  4.42 us
    dot_general x1, matrix products, attend(): jnp.einsum('lhfg,glhe->flhe', attn_probs, values, preferred_element_type=...  3.49 us
  transfers between devices with their start and end apart: 3, of which 1 were waited for; matrix products, arithmetic and copies ran while one was open for 28% of the time, Pallas kernels for 0%

profile of v1, /device:TPU:0, one launch (start us, length us, event | category | flops | bytes accessed | tf_op | source)
XLA Modules:
  0.0 139.9 jit_solution(13695072113758830949)
XLA Ops:
  6.5 0.0 copy-start
  6.5 0.0 all-gather.3.cloned.1.call-start
  6.5 0.7 all-gather.3.cloned.1.call-update
  7.3 1.7 %bitcast_dynamic-update-slice_fusion.7 = bf16[8,1,3,32,1280]{4,3,2,1,0:T(8,128)(2,1)} fusion(bf16[1,3,256,1280]{3,2,1,0:T(8,128)(2,1)} %param.5), kind=kLoop, calls=%fused_computation.28 | loop fusion | bytes 491520
  8.9 1.7 %bitcast_dynamic-update-slice_fusion.6 = bf16[8,1,3,32,1280]{4,3,2,1,0:T(8,128)(2,1)} fusion(bf16[8,1,3,32,1280]{4,3,2,1,0:T(8,128)(2,1)} %bitcast_dynamic-update-slice_fusion.7, bf16[1,3,256,1280]{3,2,1,0:T(8,128)(2,1)} %param.5), kind=kLoop, calls=%fused_computation.27 | loop fusion | bytes 491520
  10.6 0.0 copy-done
  10.6 0.7 bitcast_dynamic-update-slice_fusion.5
  11.3 0.7 bitcast_dynamic-update-slice_fusion.4
  12.0 0.7 bitcast_dynamic-update-slice_fusion.3
  12.7 0.7 bitcast_dynamic-update-slice_fusion.2
  13.4 0.7 bitcast_dynamic-update-slice_fusion.1
  14.1 0.7 bitcast_dynamic-update-slice_fusion
  14.8 0.0 copy-start.3
  14.8 7.4 %all-to-all-start = ((bf16[8,1,3,32,1280]{4,3,2,1,0:T(8,128)(2,1)}), bf16[8,1,3,32,1280]{4,3,2,1,0:T(8,128)(2,1)S(1)}, u32[]{:S(2)}, u32[]{:S(2)}) async-start(bf16[8,1,3,32,1280]{4,3,2,1,0:T(8,128)(2,1)} %bitcast_dynamic-update-slice_fusion), calls=%async_computation | async-start | bytes 3932160 | tf_op jit(solution)/shard_map/all_to_all | solution.py:45
  22.3 0.0 all-gather.5.cloned.1.call-start
  22.3 0.7 all-gather.5.cloned.1.call-update
  23.0 0.0 copy-done.3
  23.0 0.1 broadcast_compare_fusion
  23.1 0.0 copy-start.2
  23.1 44.6 %all-to-all-done = bf16[8,1,3,32,1280]{4,3,2,1,0:T(8,128)(2,1)S(1)} async-done(((bf16[8,1,3,32,1280]{4,3,2,1,0:T(8,128)(2,1)}), bf16[8,1,3,32,1280]{4,3,2,1,0:T(8,128)(2,1)S(1)}, u32[]{:S(2)}, u32[]{:S(2)}) %all-to-all-start) | async-done | bytes 1966112 | tf_op jit(solution)/shard_map/all_to_all | solution.py:45
  67.7 0.3 convert_reduce_fusion
  68.0 0.1 div.17
  68.1 0.7 multiply_reduce_fusion
  68.8 0.1 rsqrt.12
  68.9 0.0 copy-done.2
  68.9 1.9 %fusion.2 = bf16[768,1280]{1,0:T(8,128)(2,1)} fusion(bf16[8,1,3,32,1280]{4,3,2,1,0:T(8,128)(2,1)S(1)} %all-to-all-done, f32[1280]{0:T(1024)S(1)} %copy-done.2, f32[768]{0:T(1024)S(1)} %rsqrt.12, f32[768]{0:T(1024)S(1)} %div.17), kind=kLoop, calls=%fused_computation.4 | loop fusion | flops 4915200 | bytes 3943424 | tf_op jit(solution)/shard_map/convert_element_type | solution.py:17
  70.8 0.0 all-gather.3.cloned.1.call-done
  70.8 9.8 %fusion.17 = (bf16[768,1920]{1,0:T(8,128)(2,1)S(1)}, f32[768,1920]{1,0:T(8,128)}) fusion(bf16[768,1280]{1,0:T(8,128)(2,1)} %fusion.2, bf16[1280,1920]{0,1:T(8,128)(2,1)} %all-gather.3.cloned.1.call-done), kind=kOutput, calls=%fused_computation.34 | convolution fusion | flops 3776348160 | bytes 15728640 | tf_op jit(solution)/shard_map/dot_general | solution.py:51
  80.6 0.2 fusion.16
  80.8 1.6 %reshape.89 = bf16[24,32,8,80]{3,2,1,0:T(8,128)(2,1)S(1)} reshape(bf16[768,640]{1,0:T(8,128)(2,1)S(1)} %get-tuple-element.6) | data formatting | bytes 1966080 | tf_op jit(solution)/shard_map/reshape | solution.py:58
  82.4 1.7 %fusion.5 = bf16[768,640]{1,0:T(8,128)(2,1)S(1)} fusion(f32[768,1920]{1,0:T(8,128)} %get-tuple-element.8), kind=kLoop, calls=%fused_computation.11 | loop fusion | flops 983040 | bytes 2949120 | tf_op jit(solution)/shard_map/convert_element_type | solution.py:21
  84.1 2.5 %reshape.88 = bf16[24,32,8,80]{3,2,1,0:T(8,128)(2,1)} reshape(bf16[768,640]{1,0:T(8,128)(2,1)S(1)} %fusion.5) | data formatting | bytes 1966080 | tf_op jit(solution)/shard_map/reshape | solution.py:58
  86.6 5.7 %fusion.4 = (f32[32,8,24]{2,1,0:T(8,128)S(1)}, f32[32,8,24,24]{2,3,1,0:T(8,128)}) fusion(pred[24,24]{0,1:T(8,128)(4,1)S(1)} %broadcast_compare_fusion, bf16[24,32,8,80]{3,2,1,0:T(8,128)(2,1)S(1)} %reshape.89, bf16[24,32,8,80]{3,2,1,0:T(8,128)(2,1)} %reshape.88), kind=kOutput, calls=%fused_computation.9 | convolution fusion | flops 23881728 | bytes 2581056 | tf_op jit(solution)/shard_map/flhe,glhe->lhfg/dot_general | solution.py:28
  92.3 1.6 %reshape.87 = bf16[24,32,8,80]{3,2,1,0:T(8,128)(2,1)S(1)} reshape(bf16[768,640]{1,0:T(8,128)(2,1)S(1)} %get-tuple-element.5) | data formatting | bytes 1966080 | tf_op jit(solution)/shard_map/reshape | solution.py:58
  94.0 3.5 %fusion.12 = bf16[24,32,8,80]{3,0,2,1:T(8,128)(2,1)S(1)} fusion(f32[32,8,24,24]{2,3,1,0:T(8,128)} %get-tuple-element.10, f32[32,8,24]{2,1,0:T(8,128)S(1)} %get-tuple-element.9, pred[24,24]{0,1:T(8,128)(4,1)S(1)} %broadcast_compare_fusion, bf16[24,32,8,80]{3,2,1,0:T(8,128)(2,1)S(1)} %reshape.87), kind=kOutput, calls=%fused_computation.20 | convolution fusion | flops 24526848 | bytes 2581056 | tf_op jit(solution)/shard_map/lhfg,glhe->flhe/dot_general | solution.py:32
  97.5 0.3 copy.26
  97.8 1.2 reshape.90
  99.0 28.1 %all_to_all.20 = bf16[1,24,32,640]{3,2,0,1:T(8,128)(2,1)S(1)} all-to-all(bf16[1,24,32,640]{3,2,0,1:T(8,128)(2,1)S(1)} %bitcast.41), channel_id=1, replica_groups=mesh['dp'=4,'seq'=8] {'seq'}, dimensions={1} | all-to-all | bytes 1966080 | tf_op jit(solution)/shard_map/all_to_all | solution.py:60
  127.1 0.0 copy-start.1
  127.1 0.1 copy.28
  127.2 0.0 all-gather.5.cloned.1.call-done
  127.2 1.4 %copy-done.1 = bf16[1,3,256,1280]{3,2,1,0:T(8,128)(2,1)S(1)} copy-done((bf16[1,3,256,1280]{3,2,1,0:T(8,128)(2,1)S(1)}, bf16[1,3,256,1280]{3,2,1,0:T(8,128)(2,1)}, u32[]{:S(2)}) %copy-start.1) | copy-done | bytes 1966104
  128.6 4.4 %fusion.3 = bf16[768,1280]{1,0:T(8,128)(2,1)} fusion(bf16[768,640]{1,0:T(8,128)(2,1)S(1)} %bitcast.44, bf16[640,1280]{0,1:T(8,128)(2,1)} %all-gather.5.cloned.1.call-done, bf16[768,1280]{1,0:T(8,128)(2,1)S(1)} %bitcast.43), kind=kOutput, calls=%fused_computation.6 | convolution fusion | flops 1261240320 | bytes 6553600 | tf_op jit(solution)/shard_map/dot_general | solution.py:67
  (2 shorter events, 0.0 us)
Async XLA Ops:
  6.5 4.0 %copy-start = (bf16[1,3,256,1280]{3,2,1,0:T(8,128)(2,1)S(1)}, bf16[1,3,256,1280]{3,2,1,0:T(8,128)(2,1)}, u32[]{:S(2)}) copy-start(bf16[1,3,256,1280]{3,2,1,0:T(8,128)(2,1)} %param.5) | copy-start | bytes 5898244
  6.5 64.3 %all-gather.3.cloned.1.call-start = ((), (), s32[]{:S(2)}) async-start(), calls=%async_computation.2 | async-start | bytes 6144000 | tf_op jit(solution)/shard_map/all_gather | solution.py:54
  14.8 8.2 %copy-start.3 = (s32[1,24]{1,0:T(1,128)S(1)}, s32[1,24]{1,0:T(1,128)}, u32[]{:S(2)}) copy-start(s32[1,24]{1,0:T(1,128)} %param.6) | copy-start | bytes 292
  14.8 52.8 %all-to-all-start = ((bf16[8,1,3,32,1280]{4,3,2,1,0:T(8,128)(2,1)}), bf16[8,1,3,32,1280]{4,3,2,1,0:T(8,128)(2,1)S(1)}, u32[]{:S(2)}, u32[]{:S(2)}) async-start(bf16[8,1,3,32,1280]{4,3,2,1,0:T(8,128)(2,1)} %bitcast_dynamic-update-slice_fusion), calls=%async_computation | async-start | bytes 3932160 | tf_op jit(solution)/shard_map/all_to_all | solution.py:45
  22.3 105.0 %all-gather.5.cloned.1.call-start = ((), (), s32[]{:S(2)}) async-start(), calls=%async_computation.3 | async-start | bytes 2048000 | tf_op jit(solution)/shard_map/all_gather | solution.py:69
  23.1 45.8 %copy-start.2 = (f32[1280]{0:T(1024)S(1)}, f32[1280]{0:T(1024)}, u32[]{:S(2)}) copy-start(f32[1280]{0:T(1024)} %param.7) | copy-start | bytes 15364
  127.1 1.5 %copy-start.1 = (bf16[1,3,256,1280]{3,2,1,0:T(8,128)(2,1)S(1)}, bf16[1,3,256,1280]{3,2,1,0:T(8,128)(2,1)}, u32[]{:S(2)}) copy-start(bf16[1,3,256,1280]{3,2,1,0:T(8,128)(2,1)} %param.5) | copy-start | bytes 5898244
Sparse Core Ops, SparseCore 0:
  8.9 41.2 all-gather.2
  51.8 19.9 all-gather.4
